TPU v7x, 32 devices: a whole 2x2x4 slice. The times are simulated.
32 devices in a mesh: view: 2 (over y), row: 2 (over x), col: 8 (over z, core).
Axes of the slice: x: 2, y: 2, z: 4, core: 2. Of those that a mesh axis runs over, the one named last changes fastest.
Arguments:
- inputs: bfloat16 [2, 512, 8192], P('view', 'col', 'row'), may hold values from -28 to 28, as said below
- weight: bfloat16 [8192, 8192], P('row', 'col'), may hold values from -0.0625 to 0.0625
Outputs:
- grad_hidden: bfloat16 [2, 512, 8192], P('view', 'col', 'row')
- grad_weight: float32 [8192, 8192], P('row', 'col')
Inputs may be any that keep to these rules, and one draw needn't show every extreme that they name: `inputs`: feature activations of the two views of a clip; each feature has its own scale.
All inputs are finite; a program needn't handle non-finite values.
Results may differ from a plain program's by a relative error of at most 0.025.
Values may be sent and summed in bfloat16 or wider, within the bound.
No kernel may reach another device: no remote copies, remote signals or barrier semaphores. Data moves between devices by JAX's collectives and lax.ppermute only.
A program may use at most 128 MiB of HBM per device.

v0:
```python
import math
import jax
import jax.numpy as jnp
from jax import lax
from jax.sharding import PartitionSpec as P

off_weight = 0.0051
norm_eps = 1e-05


def from_partner(block, axis, distance):
    count = lax.axis_size(axis)
    route = []
    for low in range(count):
        high = low | 1 << distance
        if high != low and high < count:
            route += [(low, high), (high, low)]
    return lax.ppermute(block, axis, route)


def shards(inputs, weight):
    hidden = lax.all_gather(inputs[0], "col", axis=0, tiled=True)
    batch = hidden.shape[0]
    columns = weight
    pre = lax.psum_scatter(
        lax.dot_general(
            columns, hidden, (((0,), (1,)), ((), ())), preferred_element_type=jnp.float32
        ).astype(jnp.bfloat16),
        "row",
        scatter_dimension=0,
        tiled=True,
    ).astype(jnp.float32)
    centred = pre - jnp.mean(pre, axis=1, keepdims=True)
    rstd = lax.rsqrt(jnp.mean(centred * centred, axis=1, keepdims=True) + norm_eps)
    own = (centred * rstd).astype(jnp.bfloat16)
    partner = from_partner(own, "view", 0)
    own_f = own.astype(jnp.float32)
    partner_f = partner.astype(jnp.float32)
    diag = jnp.sum(own_f * partner_f, axis=1, keepdims=True) / batch
    piece = lax.all_gather(partner, ("row", "col"), axis=0, tiled=True)
    corr = (
        lax.dot_general(own, piece, (((1,), (1,)), ((), ())), preferred_element_type=jnp.float32)
        / batch
    )
    mixed = jnp.dot(corr.astype(jnp.bfloat16), piece, preferred_element_type=jnp.float32)
    scale_diag = 2.0 * (diag - 1.0) - 2.0 * off_weight * diag
    dnorm = 2.0 * off_weight * mixed + scale_diag * partner_f
    inner = jnp.mean(dnorm * own_f, axis=1, keepdims=True)
    dpre = (rstd * (dnorm - jnp.mean(dnorm, axis=1, keepdims=True) - own_f * inner)).astype(
        jnp.bfloat16
    )
    grads = lax.all_gather(dpre, "row", axis=0, tiled=True)
    local_weight = lax.dot_general(
        hidden, grads, (((0,), (1,)), ((), ())), preferred_element_type=jnp.float32
    )
    grad_weight = lax.psum(local_weight.astype(jnp.bfloat16), "view").astype(
        jnp.float32
    ) / math.sqrt(2.0 * batch)
    columns = grads
    grad_hidden = lax.psum_scatter(
        lax.dot_general(
            columns, weight, (((0,), (1,)), ((), ())), preferred_element_type=jnp.float32
        ).astype(jnp.bfloat16),
        "col",
        scatter_dimension=0,
        tiled=True,
    )
    return (grad_hidden[None], grad_weight)


def solution(mesh):
    return jax.shard_map(
        shards,
        mesh=mesh,
        in_specs=(P("view", "col", "row"), P("row", "col")),
        out_specs=(P("view", "col", "row"), P("row", "col")),
        check_vma=False,
    )
```

profile of v0, /device:TPU:0, one launch (start us, length us, event | category | flops | bytes accessed | tf_op | source)
XLA Modules:
  0.0 486.3 jit_solution(11138176716313369393)
XLA Ops:
  7.2 0.0 all-gather.9.cloned.1.call-start
  7.2 0.7 all-gather.9.cloned.1.call-update
  7.9 0.0 reduce-scatter.3.cloned.1.call-start
  7.9 51.2 %all-gather.9.cloned.1.call-done = bf16[1,512,4096]{2,1,0:T(8,128)(2,1)} async-done(((bf16[1,64,4096]{2,1,0:T(8,128)(2,1)}), bf16[1,512,4096]{2,1,0:T(8,128)(2,1)}) %all-gather.9.cloned.1.call-update) | async-done | bytes 4194320 | tf_op jit(solution)/shard_map/all_gather | solution.py:22
  59.2 10.1 %fusion.4 = bf16[1024,512]{1,0:T(8,128)(2,1)} fusion(bf16[4096,1024]{1,0:T(8,128)(2,1)} %param.3, bf16[1,512,4096]{2,1,0:T(8,128)(2,1)} %all-gather.9.cloned.1.call-done), kind=kOutput, calls=%fused_computation.11 | convolution fusion | flops 4295491584 | bytes 13631488 | tf_op jit(solution)/shard_map/dot_general | solution.py:26
  69.3 0.0 reduce-scatter.3.cloned.1.call-update
  69.3 0.0 all-gather.5.cloned.1.call-start
  69.4 19.3 %reduce-scatter.3.cloned.1.call-done = bf16[512,512]{1,0:T(8,128)(2,1)} async-done(((bf16[1024,512]{1,0:T(8,128)(2,1)}), bf16[512,512]{1,0:T(8,128)(2,1)}) %reduce-scatter.3.cloned.1.call-update) | async-done | bytes 524304 | tf_op jit(solution)/shard_map/reduce_scatter | solution.py:25
  88.7 1.2 convert_reduce_fusion
  89.9 1.3 fusion.11
  91.2 1.3 fusion.12
  92.5 1.5 collective-permute-start
  94.0 12.0 %collective-permute-done = bf16[512,512]{1,0:T(8,128)(2,1)S(1)} collective-permute-done((bf16[512,512]{1,0:T(8,128)(2,1)S(1)}, bf16[512,512]{1,0:T(8,128)(2,1)S(1)}, u32[]{:S(2)}, u32[]{:S(2)}) %collective-permute-start) | collective-permute-done | bytes 524320 | tf_op jit(solution)/shard_map/ppermute | solution.py:18
  106.0 0.0 copy-start.1
  106.0 0.8 copy-done.1
  106.8 0.0 all-gather.5.cloned.1.call-update
  106.8 0.0 all-gather.7.cloned.1.call-start
  106.9 1.6 fusion.13
  108.5 0.0 copy-start
  108.6 72.7 %all-gather.5.cloned.1.call-done = bf16[8192,512]{1,0:T(8,128)(2,1)} async-done(((bf16[512,512]{1,0:T(8,128)(2,1)}), bf16[8192,512]{1,0:T(8,128)(2,1)}) %all-gather.5.cloned.1.call-update) | async-done | bytes 8388624 | tf_op jit(solution)/shard_map/all_gather | solution.py:40
  181.3 15.2 %fusion.19 = (f32[512]{0:T(512)S(1)}, f32[512]{0:T(512)S(1)}, f32[512,512]{1,0:T(8,128)S(1)}) fusion(bf16[512,512]{1,0:T(8,128)(2,1)S(1)} %fusion.12, bf16[512,512]{1,0:T(8,128)(2,1)} %copy-done.1, f32[512]{0:T(512)S(1)} %multiply_subtract_fusion, bf16[8192,512]{1,0:T(8,128)(2,1)} %all-gather.5.cloned.1.call-done), kind=kOutput, calls=%fused_computation.32 | convolution fusion | flops 8600420352 | bytes 10491904 | tf_op jit(solution)/shard_map/dot_general | solution.py:45
  196.5 0.0 copy-done
  196.6 1.1 fusion.17
  197.7 0.0 all-gather.7.cloned.1.call-update
  197.7 0.2 all-reduce.2.cloned.1.call-start
  197.9 19.8 %all-gather.7.cloned.1.call-done = bf16[1024,512]{1,0:T(8,128)(2,1)} async-done(((bf16[512,512]{1,0:T(8,128)(2,1)}), bf16[1024,512]{1,0:T(8,128)(2,1)}) %all-gather.7.cloned.1.call-update) | async-done | bytes 1048592 | tf_op jit(solution)/shard_map/all_gather | solution.py:52
  217.7 10.4 %convert_bitcast_fusion = bf16[4096,1024]{0,1:T(8,128)(2,1)} fusion(bf16[1024,512]{1,0:T(8,128)(2,1)} %all-gather.7.cloned.1.call-done, bf16[1,512,4096]{2,1,0:T(8,128)(2,1)} %all-gather.9.cloned.1.call-done), kind=kOutput, calls=%fused_computation.2 | convolution fusion | flops 4299161600 | bytes 13631488 | tf_op jit(solution)/shard_map/dot_general | solution.py:53
  228.2 0.0 copy-start.2
  228.2 0.0 all-reduce.2.cloned.1.call-update
  228.2 0.0 reduce-scatter.5.cloned.1.call-start
  228.2 1.1 copy-done.2
  229.4 9.6 %convolution_convert_fusion = bf16[512,4096]{1,0:T(8,128)(2,1)} fusion(bf16[1024,512]{1,0:T(8,128)(2,1)S(1)} %copy-done.2, bf16[4096,1024]{1,0:T(8,128)(2,1)} %param.3), kind=kOutput, calls=%fused_computation.3 | convolution fusion | flops 4297064448 | bytes 13631488 | tf_op jit(solution)/shard_map/dot_general | solution.py:61
  239.0 0.0 reduce-scatter.5.cloned.1.call-update
  239.0 187.4 %all-reduce.2.cloned.1.call-done = bf16[4096,1024]{0,1:T(8,128)(2,1)} async-done(((bf16[4096,1024]{0,1:T(8,128)(2,1)}), bf16[4096,1024]{0,1:T(8,128)(2,1)}) %all-reduce.2.cloned.1.call-update) | async-done | bytes 8388624 | tf_op jit(solution)/shard_map/psum | solution.py:56
  426.4 11.7 %convert_multiply_fusion = f32[4096,1024]{0,1:T(8,128)} fusion(bf16[4096,1024]{0,1:T(8,128)(2,1)} %all-reduce.2.cloned.1.call-done), kind=kLoop, calls=%fused_computation | loop fusion | flops 8388608 | bytes 25165824 | tf_op jit(solution)/shard_map/div | solution.py:56
  438.1 17.5 %copy.5 = f32[4096,1024]{1,0:T(8,128)} copy(f32[4096,1024]{0,1:T(8,128)} %convert_multiply_fusion) | data formatting | bytes 33554432
  455.6 23.8 %reduce-scatter.5.cloned.1.call-done = bf16[64,4096]{1,0:T(8,128)(2,1)} async-done(((bf16[512,4096]{1,0:T(8,128)(2,1)}), bf16[64,4096]{1,0:T(8,128)(2,1)}) %reduce-scatter.5.cloned.1.call-update) | async-done | bytes 524304 | tf_op jit(solution)/shard_map/reduce_scatter | solution.py:60
  (4 shorter events, 0.0 us)
Async XLA Ops:
  7.2 52.0 %all-gather.9.cloned.1.call-start = ((), (), s32[]{:S(2)}) async-start(), calls=%async_computation.7 | async-start | bytes 4718592 | tf_op jit(solution)/shard_map/all_gather | solution.py:22
  7.9 80.8 %reduce-scatter.3.cloned.1.call-start = ((), (), s32[]{:S(2)}) async-start(), calls=%async_computation.2 | async-start | bytes 1572864 | tf_op jit(solution)/shard_map/reduce_scatter | solution.py:25
  69.3 112.0 %all-gather.5.cloned.1.call-start = ((), (), s32[]{:S(2)}) async-start(), calls=%async_computation.3 | async-start | bytes 8912896 | tf_op jit(solution)/shard_map/all_gather | solution.py:40
  92.5 13.6 %collective-permute-start = (bf16[512,512]{1,0:T(8,128)(2,1)S(1)}, bf16[512,512]{1,0:T(8,128)(2,1)S(1)}, u32[]{:S(2)}, u32[]{:S(2)}) collective-permute-start(bf16[512,512]{1,0:T(8,128)(2,1)S(1)} %fusion.12), channel_id=1, source_target_pairs={{0,16},{16,0},{1,17},{17,1},{2,18},{18,2},{3,19},{19,3},{4,20},{20... | collective-permute-start | bytes 1572872 | tf_op jit(solution)/shard_map/ppermute | solution.py:18
  106.0 0.8 copy-start.1
  106.8 110.9 %all-gather.7.cloned.1.call-start = ((), (), s32[]{:S(2)}) async-start(), calls=%async_computation.4 | async-start | bytes 1572864 | tf_op jit(solution)/shard_map/all_gather | solution.py:52
  108.5 88.0 %copy-start = (bf16[512,512]{1,0:T(8,128)(2,1)S(1)}, bf16[512,512]{1,0:T(8,128)(2,1)}, u32[]{:S(2)}) copy-start(bf16[512,512]{1,0:T(8,128)(2,1)} %reduce-scatter.3.cloned.1.call-done) | copy-start | bytes 1572868
  197.7 228.7 %all-reduce.2.cloned.1.call-start = ((), (), s32[]{:S(2)}) async-start(), calls=%async_computation.6 | async-start | bytes 16777216 | tf_op jit(solution)/shard_map/psum | solution.py:56
  228.2 1.2 copy-start.2
  228.2 251.2 %reduce-scatter.5.cloned.1.call-start = ((), (), s32[]{:S(2)}) async-start(), calls=%async_computation.5 | async-start | bytes 4718592 | tf_op jit(solution)/shard_map/reduce_scatter | solution.py:60
Sparse Core Ops, SparseCore 0:
  9.6 49.5 all-gather.8
  69.4 19.1 reduce-scatter.2
  107.0 74.2 all-gather.4
  197.8 19.8 all-gather.6
  228.3 198.0 all-reduce.1
  429.1 50.2 reduce-scatter.4
where the time goes:
time: 487 us; the launch traced here: 486 us
  waiting for transfers between devices  387 us (79%)
  matrix products  45.4 us (9%)
  local copies, waits for them, and re-layouts  19.5 us (4%)
  other arithmetic  18.3 us (4%)
  between operations  14.2 us (3%)
    psum x1, waiting for transfers between devices, shards(): lax.psum(local_weight.astype(jnp.bfloat16), 'view').astype(jnp.float32)  187 us
    all_gather x1, waiting for transfers between devices, shards(): piece = lax.all_gather(partner, ('row', 'col'), axis=0, tiled=True)  72.7 us
    all_gather x1, waiting for transfers between devices, shards(): hidden = lax.all_gather(inputs[0], 'col', axis=0, tiled=True)  51.2 us
    reduce_scatter x1, waiting for transfers between devices, shards(): lax.psum_scatter(lax.dot_general(columns, weight, (((0,), (1,)), ((), ())...  23.8 us
    all_gather x1, waiting for transfers between devices, shards(): grads = lax.all_gather(dpre, 'row', axis=0, tiled=True)  19.8 us
    unnamed x7, local copies, waits for them, and re-layouts  19.5 us
    reduce_scatter x1, waiting for transfers between devices, shards(): lax.psum_scatter(lax.dot_general(columns, hidden, (((0,), (1,)), ((), ())...  19.3 us
    dot_general x1, matrix products, shards(): jnp.dot(corr.astype(jnp.bfloat16), piece, preferred_element_type=jnp.floa...  15.2 us
  transfers between devices with their start and end apart: 7, of which 7 were waited for; matrix products, arithmetic and copies ran while one was open for 8% of the time, Pallas kernels for 0%

commit v1 on v0

--- a/solution.py
+++ b/solution.py
@@ -19,7 +19,9 @@
 
 
 def shards(inputs, weight):
-    hidden = lax.all_gather(inputs[0], "col", axis=0, tiled=True)
+    hidden = jnp.concatenate(
+        lax.all_to_all(jnp.stack([inputs[0]] * lax.axis_size("col")), "col", 0, 0), axis=0
+    )
     batch = hidden.shape[0]
     columns = weight
     pre = lax.psum_scatter(

time: 487 us -> 534 us (1.097)
  blocking collectives: 0 us -> 100 us
  waiting for transfers between devices: 387 us -> 335 us
    all_to_all x0 -> x1, blocking collectives: none -> 100 us  [shards(): lax.all_to_all(jnp.stack([inputs[0]] * lax.axis_size('col')), 'col', 0, 0)]
    all_gather x1 -> x0, waiting for transfers between devices: 51.2 us -> none  [shards(): hidden = lax.all_gather(inputs[0], 'col', axis=0, tiled=True)]
    unnamed x7 -> x11, local copies, waits for them, and re-layouts: 19.5 us -> 21.5 us
  transfers between devices with their start and end apart: 7 -> 6, of which waited for: 7 -> 6; matrix products, arithmetic and copies ran while one was open for 8% -> 8% of each run, Pallas kernels for 0% -> 0%
where the time goes in v1:
time: 534 us
  waiting for transfers between devices  335 us (63%)
  blocking collectives  100 us (19%)
  matrix products  40.8 us (8%)
  local copies, waits for them, and re-layouts  23.2 us (4%)
  other arithmetic  18.3 us (3%)
  between operations  13.9 us (3%)
    psum x1, waiting for transfers between devices, shards(): lax.psum(local_weight.astype(jnp.bfloat16), 'view').astype(jnp.float32)  187 us
    all_to_all x1, blocking collectives, shards(): lax.all_to_all(jnp.stack([inputs[0]] * lax.axis_size('col')), 'col', 0, 0)  100 us
    all_gather x1, waiting for transfers between devices, shards(): piece = lax.all_gather(partner, ('row', 'col'), axis=0, tiled=True)  72.7 us
    reduce_scatter x1, waiting for transfers between devices, shards(): lax.psum_scatter(lax.dot_general(columns, weight, (((0,), (1,)), ((), ())...  23.8 us
    unnamed x11, local copies, waits for them, and re-layouts  21.5 us
    all_gather x1, waiting for transfers between devices, shards(): grads = lax.all_gather(dpre, 'row', axis=0, tiled=True)  19.8 us
    reduce_scatter x1, waiting for transfers between devices, shards(): lax.psum_scatter(lax.dot_general(columns, hidden, (((0,), (1,)), ((), ())...  19.4 us
    dot_general x1, matrix products, shards(): jnp.dot(corr.astype(jnp.bfloat16), piece, preferred_element_type=jnp.floa...  15.2 us
  transfers between devices with their start and end apart: 6, of which 6 were waited for; matrix products, arithmetic and copies ran while one was open for 8% of the time, Pallas kernels for 0%

profile of v1, /device:TPU:0, one launch (start us, length us, event | category | flops | bytes accessed | tf_op | source)
XLA Modules:
  0.0 533.6 jit_solution(7468107121343447456)
XLA Ops:
  7.2 0.0 reduce-scatter.3.cloned.1.call-start
  7.2 0.0 copy-start.3
  7.2 1.7 stack.3
  8.9 100.4 %all_to_all.5 = bf16[8,64,4096]{2,1,0:T(8,128)(2,1)S(1)} all-to-all(bf16[8,64,4096]{2,1,0:T(8,128)(2,1)S(1)} %stack.3), channel_id=1, replica_groups=mesh['view'=2,'row'=2,'col'=8] {'col'}, dimensions={0} | all-to-all | bytes 8388608 | tf_op jit(solution)/shard_map/all_to_all | solution.py:23
  109.3 0.0 copy-start.1
  109.3 2.0 copy-done.1
  111.3 0.0 copy-done.3
  111.3 5.5 %convolution_convert_fusion.1 = bf16[1024,512]{1,0:T(8,128)(2,1)} fusion(bf16[4096,1024]{1,0:T(8,128)(2,1)S(1)} %copy-done.3, bf16[512,4096]{1,0:T(8,128)(2,1)S(1)} %bitcast.14), kind=kOutput, calls=%fused_computation.8 | convolution fusion | flops 4295491584 | bytes 13631488 | tf_op jit(solution)/shard_map/dot_general | solution.py:28
  116.8 0.0 reduce-scatter.3.cloned.1.call-update
  116.8 0.0 all-gather.3.cloned.1.call-start
  116.9 19.4 %reduce-scatter.3.cloned.1.call-done = bf16[512,512]{1,0:T(8,128)(2,1)} async-done(((bf16[1024,512]{1,0:T(8,128)(2,1)}), bf16[512,512]{1,0:T(8,128)(2,1)}) %reduce-scatter.3.cloned.1.call-update) | async-done | bytes 524304 | tf_op jit(solution)/shard_map/reduce_scatter | solution.py:27
  136.3 1.2 convert_reduce_fusion
  137.5 1.3 fusion.5
  138.9 1.3 fusion.6
  140.1 1.6 collective-permute-start
  141.7 12.0 %collective-permute-done = bf16[512,512]{1,0:T(8,128)(2,1)S(1)} collective-permute-done((bf16[512,512]{1,0:T(8,128)(2,1)S(1)}, bf16[512,512]{1,0:T(8,128)(2,1)S(1)}, u32[]{:S(2)}, u32[]{:S(2)}) %collective-permute-start) | collective-permute-done | bytes 524320 | tf_op jit(solution)/shard_map/ppermute | solution.py:18
  153.7 0.0 copy-start.2
  153.7 0.8 copy-done.2
  154.5 0.0 all-gather.3.cloned.1.call-update
  154.5 0.0 all-gather.5.cloned.1.call-start
  154.6 1.6 fusion.7
  156.2 0.0 copy-start
  156.2 72.7 %all-gather.3.cloned.1.call-done = bf16[8192,512]{1,0:T(8,128)(2,1)} async-done(((bf16[512,512]{1,0:T(8,128)(2,1)}), bf16[8192,512]{1,0:T(8,128)(2,1)}) %all-gather.3.cloned.1.call-update) | async-done | bytes 8388624 | tf_op jit(solution)/shard_map/all_gather | solution.py:42
  229.0 15.2 %fusion.13 = (f32[512]{0:T(512)S(1)}, f32[512]{0:T(512)S(1)}, f32[512,512]{1,0:T(8,128)S(1)}) fusion(bf16[512,512]{1,0:T(8,128)(2,1)S(1)} %fusion.6, bf16[512,512]{1,0:T(8,128)(2,1)} %copy-done.2, f32[512]{0:T(512)S(1)} %multiply_subtract_fusion, bf16[8192,512]{1,0:T(8,128)(2,1)} %all-gather.3.cloned.1.call-done), kind=kOutput, calls=%fused_computation.29 | convolution fusion | flops 8600420352 | bytes 10491904 | tf_op jit(solution)/shard_map/dot_general | solution.py:47
  244.2 0.0 copy-done
  244.2 1.1 fusion.11
  245.4 0.0 all-gather.5.cloned.1.call-update
  245.4 0.2 all-reduce.2.cloned.1.call-start
  245.6 19.8 %all-gather.5.cloned.1.call-done = bf16[1024,512]{1,0:T(8,128)(2,1)} async-done(((bf16[512,512]{1,0:T(8,128)(2,1)}), bf16[1024,512]{1,0:T(8,128)(2,1)}) %all-gather.5.cloned.1.call-update) | async-done | bytes 1048592 | tf_op jit(solution)/shard_map/all_gather | solution.py:54
  265.4 10.4 %convert_bitcast_fusion = bf16[4096,1024]{0,1:T(8,128)(2,1)} fusion(bf16[1024,512]{1,0:T(8,128)(2,1)} %all-gather.5.cloned.1.call-done, bf16[512,4096]{1,0:T(8,128)(2,1)} %bitcast.15), kind=kOutput, calls=%fused_computation.2 | convolution fusion | flops 4299161600 | bytes 13631488 | tf_op jit(solution)/shard_map/dot_general | solution.py:55
  275.9 0.0 copy-start.4
  275.9 0.0 all-reduce.2.cloned.1.call-update
  275.9 0.0 reduce-scatter.5.cloned.1.call-start
  275.9 1.1 copy-done.4
  277.1 9.6 %convolution_convert_fusion = bf16[512,4096]{1,0:T(8,128)(2,1)} fusion(bf16[1024,512]{1,0:T(8,128)(2,1)S(1)} %copy-done.4, bf16[4096,1024]{1,0:T(8,128)(2,1)} %param.3), kind=kOutput, calls=%fused_computation.3 | convolution fusion | flops 4297064448 | bytes 13631488 | tf_op jit(solution)/shard_map/dot_general | solution.py:63
  286.7 0.0 reduce-scatter.5.cloned.1.call-update
  286.7 187.4 %all-reduce.2.cloned.1.call-done = bf16[4096,1024]{0,1:T(8,128)(2,1)} async-done(((bf16[4096,1024]{0,1:T(8,128)(2,1)}), bf16[4096,1024]{0,1:T(8,128)(2,1)}) %all-reduce.2.cloned.1.call-update) | async-done | bytes 8388624 | tf_op jit(solution)/shard_map/psum | solution.py:58
  474.1 11.7 %convert_multiply_fusion = f32[4096,1024]{0,1:T(8,128)} fusion(bf16[4096,1024]{0,1:T(8,128)(2,1)} %all-reduce.2.cloned.1.call-done), kind=kLoop, calls=%fused_computation | loop fusion | flops 8388608 | bytes 25165824 | tf_op jit(solution)/shard_map/div | solution.py:58
  485.8 17.5 %copy.5 = f32[4096,1024]{1,0:T(8,128)} copy(f32[4096,1024]{0,1:T(8,128)} %convert_multiply_fusion) | data formatting | bytes 33554432
  503.3 23.8 %reduce-scatter.5.cloned.1.call-done = bf16[64,4096]{1,0:T(8,128)(2,1)} async-done(((bf16[512,4096]{1,0:T(8,128)(2,1)}), bf16[64,4096]{1,0:T(8,128)(2,1)}) %reduce-scatter.5.cloned.1.call-update) | async-done | bytes 524304 | tf_op jit(solution)/shard_map/reduce_scatter | solution.py:62
  (4 shorter events, 0.0 us)
Async XLA Ops:
  7.2 129.2 %reduce-scatter.3.cloned.1.call-start = ((), (), s32[]{:S(2)}) async-start(), calls=%async_computation.3 | async-start | bytes 1572864 | tf_op jit(solution)/shard_map/reduce_scatter | solution.py:27
  7.2 104.1 %copy-start.3 = (bf16[4096,1024]{1,0:T(8,128)(2,1)S(1)}, bf16[4096,1024]{1,0:T(8,128)(2,1)}, u32[]{:S(2)}) copy-start(bf16[4096,1024]{1,0:T(8,128)(2,1)} %param.3) | copy-start | bytes 25165828
  109.3 2.0 copy-start.1
  116.8 112.1 %all-gather.3.cloned.1.call-start = ((), (), s32[]{:S(2)}) async-start(), calls=%async_computation.4 | async-start | bytes 8912896 | tf_op jit(solution)/shard_map/all_gather | solution.py:42
  140.1 13.6 %collective-permute-start = (bf16[512,512]{1,0:T(8,128)(2,1)S(1)}, bf16[512,512]{1,0:T(8,128)(2,1)S(1)}, u32[]{:S(2)}, u32[]{:S(2)}) collective-permute-start(bf16[512,512]{1,0:T(8,128)(2,1)S(1)} %fusion.6), channel_id=1, source_target_pairs={{0,16},{16,0},{1,17},{17,1},{2,18},{18,2},{3,19},{19,3},{4,20},{20... | collective-permute-start | bytes 1572872 | tf_op jit(solution)/shard_map/ppermute | solution.py:18
  153.7 0.8 copy-start.2
  154.5 110.9 %all-gather.5.cloned.1.call-start = ((), (), s32[]{:S(2)}) async-start(), calls=%async_computation.5 | async-start | bytes 1572864 | tf_op jit(solution)/shard_map/all_gather | solution.py:54
  156.2 88.0 %copy-start = (bf16[512,512]{1,0:T(8,128)(2,1)S(1)}, bf16[512,512]{1,0:T(8,128)(2,1)}, u32[]{:S(2)}) copy-start(bf16[512,512]{1,0:T(8,128)(2,1)} %reduce-scatter.3.cloned.1.call-done) | copy-start | bytes 1572868
  245.4 228.7 %all-reduce.2.cloned.1.call-start = ((), (), s32[]{:S(2)}) async-start(), calls=%async_computation.7 | async-start | bytes 16777216 | tf_op jit(solution)/shard_map/psum | solution.py:58
  275.9 1.2 copy-start.4
  275.9 251.2 %reduce-scatter.5.cloned.1.call-start = ((), (), s32[]{:S(2)}) async-start(), calls=%async_computation.6 | async-start | bytes 4718592 | tf_op jit(solution)/shard_map/reduce_scatter | solution.py:62
Sparse Core Ops, SparseCore 0:
  117.0 19.3 reduce-scatter.2
  154.6 74.2 all-gather.2
  245.5 19.8 all-gather.4
  276.0 198.0 all-reduce.1
  476.8 50.2 reduce-scatter.4
